TPU v7x, 256 devices: a whole 4x4x8 slice. The times are simulated.
256 devices in a mesh: tile: 32 (over x, y, core), mode: 8 (over z).
Axes of the slice: x: 4, y: 4, z: 8, core: 2. Of those that a mesh axis runs over, the one named last changes fastest.
Arguments:
- mode_shapes: bfloat16 [64, 256, 2048], P('mode', 'tile'), may hold values from -6 to 6
- stiffness: float32 [256, 2048], P('tile'), may hold values from 0.5 to 4
- node_slot: int32 [256, 2048], P('tile'), may hold values from 0 to 255, as said below
- slot_zone: int32 [32, 32, 8], replicated, may hold values from 0 to 15, as said below
Outputs:
- energy: float32 [512, 64, 64], P('tile', 'mode')
Inputs may be any that keep to these rules, and one draw needn't show every extreme that they name: `slot_zone`: for each tile and owner, the 8 zone numbers are distinct. `node_slot`: slots that no node of a tile names carry no zone's nodes.
All inputs are finite; a program needn't handle non-finite values.
Results may differ from a plain program's by a relative error of at most 0.00099.
Values may be sent and summed in bfloat16 or wider, within the bound.
No kernel may reach another device: no remote copies, remote signals or barrier semaphores. Data moves between devices by JAX's collectives and lax.ppermute only.
A program may use at most 64 MiB of HBM per device.

v0:
```python
import math
import jax
import jax.numpy as jnp
from jax import lax
from jax.sharding import PartitionSpec as P

ZONES = 512
POISSON = 0.3
SHEAR = 2.0 * (1.0 - POISSON)


def with_halo(cells, sides, width):
    for axis, dim in sides:
        count = lax.axis_size(axis)
        ends = count - 1
        head = lax.slice_in_dim(cells, 0, width, axis=dim)
        tail = lax.slice_in_dim(cells, cells.shape[dim] - width, cells.shape[dim], axis=dim)
        cells = jnp.concatenate(
            [
                lax.ppermute(tail, axis, [(i, (i + 1) % count) for i in range(ends)]),
                cells,
                lax.ppermute(head, axis, [((i + 1) % count, i) for i in range(ends)]),
            ],
            axis=dim,
        )
    return cells


def curvatures(shapes_framed):
    framed = jnp.pad(shapes_framed, ((0, 0), (0, 0), (1, 1)))
    centre = framed[:, 1:-1, 1:-1]
    along_x = framed[:, 2:, 1:-1] - 2.0 * centre + framed[:, :-2, 1:-1]
    along_y = framed[:, 1:-1, 2:] - 2.0 * centre + framed[:, 1:-1, :-2]
    twist_xy = 0.25 * (
        framed[:, 2:, 2:] - framed[:, 2:, :-2] - framed[:, :-2, 2:] + framed[:, :-2, :-2]
    )
    return jnp.stack([along_x, along_y, twist_xy]).astype(jnp.bfloat16)


def left_factor(bending, stiffness):
    along_x, along_y, twist_xy = (bending[0], bending[1], bending[2])
    return jnp.stack(
        [
            stiffness * (along_x + POISSON * along_y),
            stiffness * (along_y + POISSON * along_x),
            stiffness * (SHEAR * twist_xy),
        ]
    )


def per_device(mode_shapes, stiffness, node_slot, slot_zone):
    panel_modes, tile_rows, row_cells = mode_shapes.shape
    node_count = tile_rows * row_cells
    tile_count = lax.axis_size("tile")
    mode_count = panel_modes * lax.axis_size("mode")
    owner_slots = slot_zone.shape[2]
    slot_count = tile_count * owner_slots
    owned_zones = ZONES // tile_count
    pair_count = panel_modes * mode_count
    padded = with_halo(mode_shapes, (("tile", 1),), 1)
    own_bending = curvatures(padded.astype(jnp.float32))
    own_float = own_bending.astype(jnp.float32)
    weighted = left_factor(own_float, stiffness)
    own_sums = jnp.sum(weighted * own_float, axis=(0, 2, 3))
    placed_sums = lax.dynamic_update_slice_in_dim(
        jnp.zeros((mode_count,), jnp.float32), own_sums, lax.axis_index("mode") * panel_modes, 0
    )
    totals = 0.5 * lax.psum(placed_sums, ("tile", "mode"))
    gathered_bend = lax.all_gather(own_bending, "mode", axis=1, tiled=True)
    right_flat = gathered_bend.reshape(3, mode_count, node_count)
    left_flat = weighted.astype(jnp.bfloat16).reshape(3, panel_modes, node_count)
    slot_flat = node_slot.reshape(node_count)
    slot_range = jnp.arange(slot_count, dtype=jnp.int32)
    block_nodes = math.gcd(node_count, max(128, (1 << 20) // pair_count))

    def one_block(number, running):
        first_node = number * block_nodes
        left_block = lax.dynamic_slice_in_dim(left_flat, first_node, block_nodes, 2).astype(
            jnp.float32
        )
        right_block = lax.dynamic_slice_in_dim(right_flat, first_node, block_nodes, 2).astype(
            jnp.float32
        )
        slot_block = lax.dynamic_slice_in_dim(slot_flat, first_node, block_nodes, 0)
        products = jnp.sum(left_block[:, :, None, :] * right_block[:, None, :, :], axis=0)
        products = products.reshape(pair_count, block_nodes)
        member_block = (slot_block[:, None] == slot_range[None, :]).astype(jnp.float32)
        return running + jnp.dot(products, member_block, precision=lax.Precision.HIGHEST)

    by_pair = lax.fori_loop(
        0, node_count // block_nodes, one_block, jnp.zeros((pair_count, slot_count), jnp.float32)
    )
    routed = by_pair.T.reshape(tile_count, owner_slots, pair_count)
    tile_index = lax.axis_index("tile")
    own_lists = lax.dynamic_index_in_dim(slot_zone, tile_index, 0, keepdims=False)
    selector = (
        own_lists[:, :, None] == jnp.arange(owned_zones, dtype=jnp.int32)[None, None, :]
    ).astype(jnp.float32)
    spread_zones = jnp.einsum("dcz,dcm->dzm", selector, routed, precision=lax.Precision.HIGHEST)
    spread_zones = spread_zones.reshape(tile_count * owned_zones, pair_count)
    summed = lax.psum_scatter(spread_zones, "tile", scatter_dimension=0, tiled=True)
    own_totals = lax.dynamic_slice_in_dim(
        totals, lax.axis_index("mode") * panel_modes, panel_modes, 0
    )
    denominator = jnp.sqrt(own_totals[:, None] * totals[None, :])
    return ZONES * (0.5 * summed.reshape(owned_zones, panel_modes, mode_count)) / denominator


def solution(mesh):
    placed = (P("mode", "tile", None), P("tile", None), P("tile", None), P())
    return jax.shard_map(
        per_device, mesh=mesh, in_specs=placed, out_specs=P("tile", "mode", None), check_vma=False
    )
```

profile of v0, /device:TPU:4, one launch (start us, length us, event | category | flops | bytes accessed | tf_op | source)
XLA Modules:
  0.0 281.9 jit_solution(18030605691731812583)
XLA Ops:
  7.7 1.9 collective-permute-start
  9.6 5.8 %collective-permute-start.1 = (bf16[8,1,2048]{2,1,0:T(2,128)(2,1)S(1)}, bf16[8,1,2048]{2,1,0:T(2,128)(2,1)S(1)}, u32[]{:S(2)}, u32[]{:S(2)}) collective-permute-start(bf16[8,1,2048]{2,1,0:T(2,128)(2,1)S(1)} %get-tuple-element.161), channel_id=1, source_target_pairs={{8,0},{16,8},{24,16},{32,24},{40,32},{48,40},{56,48},{64,56},{72,6... | collective-permute-start | bytes 98312 | tf_op jit(solution)/shard_map/ppermute | solution.py:22
  15.4 1.9 collective-permute-done.1
  21.3 2.2 fusion.22
  26.8 71.7 %all-gather.2.cloned.1.call-done = bf16[3,64,8,2048]{3,2,1,0:T(8,128)(2,1)} async-done(((bf16[3,8,8,2048]{3,2,1,0:T(8,128)(2,1)}), bf16[3,64,8,2048]{3,2,1,0:T(8,128)(2,1)}) %all-gather.2.cloned.1.call-update) | async-done | bytes 6291472 | tf_op jit(solution)/shard_map/all_gather | solution.py:69
  98.5 10.4 %reshape.64 = bf16[3,64,16384]{2,1,0:T(8,128)(2,1)} reshape(bf16[3,64,8,2048]{3,2,1,0:T(8,128)(2,1)} %all-gather.2.cloned.1.call-done) | data formatting | bytes 12582912 | tf_op jit(solution)/shard_map/reshape | solution.py:70
  108.9 78.5 %while.14 = (s32[]{:T(128)}, f32[512,256]{1,0:T(8,128)S(1)}, bf16[3,8,16384]{2,1,0:T(8,128)(2,1)S(1)}, bf16[3,64,16384]{2,1,0:T(8,128)(2,1)}, s32[16384]{0:T(102...) while((s32[]{:T(128)}, f32[512,256]{1,0:T(8,128)S(1)}, bf16[3,8,16384]{2,1,0:T(8,128)(2,1)S(1)}, ...), condition=%wide.region_2.3_spmd.clone, body=%wide.region_0.0_spmd.clone.sunk | while | flops 3227697152 | bytes 13885601 | solution.py:90
  110.2 3.1 %multiply_reduce_fusion.2 = f32[8,64,2048]{2,1,0:T(8,128)} fusion(f32[3,64,2048]{2,1,0:T(8,128)S(1)} %dynamic-slice_convert_fusion.4, f32[3,8,2048]{2,1,0:T(8,128)S(1)} %dynamic-slice_convert_fusion.5), kind=kLoop, calls=%fused_computation.1.clone.1 | loop fusion | flops 5242880 | bytes 5963776 | tf_op jit(solution)/shard_map/while/body/eval_jaxpr/reduce_sum | solution.py:85
  114.0 4.7 %fusion.30 = f32[512,256]{1,0:T(8,128)S(1)} fusion(f32[512,2048]{1,0:T(8,128)} %bitcast.30, s32[2048]{0:T(1024)S(1)} %dynamic_slice.41, f32[512,256]{1,0:T(8,128)S(1)} %get-tuple-element.203, pred[]{:T(512)S(6)} %compare.4), kind=kOutput, calls=%fused_computation.4.clone.1 | convolution fusion | flops 3222011904 | bytes 5251073 | tf_op jit(solution)/shard_map/while/body/eval_jaxpr/dot_general | solution.py:88
  118.7 1.3 dynamic-slice_convert_fusion.4
  120.0 3.1 %multiply_reduce_fusion.2 = f32[8,64,2048]{2,1,0:T(8,128)} fusion(f32[3,64,2048]{2,1,0:T(8,128)S(1)} %dynamic-slice_convert_fusion.4, f32[3,8,2048]{2,1,0:T(8,128)S(1)} %dynamic-slice_convert_fusion.5), kind=kLoop, calls=%fused_computation.1.clone.1 | loop fusion | flops 5242880 | bytes 5963776 | tf_op jit(solution)/shard_map/while/body/eval_jaxpr/reduce_sum | solution.py:85
  123.8 4.7 %fusion.30 = f32[512,256]{1,0:T(8,128)S(1)} fusion(f32[512,2048]{1,0:T(8,128)} %bitcast.30, s32[2048]{0:T(1024)S(1)} %dynamic_slice.41, f32[512,256]{1,0:T(8,128)S(1)} %get-tuple-element.203, pred[]{:T(512)S(6)} %compare.4), kind=kOutput, calls=%fused_computation.4.clone.1 | convolution fusion | flops 3222011904 | bytes 5251073 | tf_op jit(solution)/shard_map/while/body/eval_jaxpr/dot_general | solution.py:88
  128.5 1.3 dynamic-slice_convert_fusion.4
  129.9 3.1 %multiply_reduce_fusion.2 = f32[8,64,2048]{2,1,0:T(8,128)} fusion(f32[3,64,2048]{2,1,0:T(8,128)S(1)} %dynamic-slice_convert_fusion.4, f32[3,8,2048]{2,1,0:T(8,128)S(1)} %dynamic-slice_convert_fusion.5), kind=kLoop, calls=%fused_computation.1.clone.1 | loop fusion | flops 5242880 | bytes 5963776 | tf_op jit(solution)/shard_map/while/body/eval_jaxpr/reduce_sum | solution.py:85
  133.6 4.7 %fusion.30 = f32[512,256]{1,0:T(8,128)S(1)} fusion(f32[512,2048]{1,0:T(8,128)} %bitcast.30, s32[2048]{0:T(1024)S(1)} %dynamic_slice.41, f32[512,256]{1,0:T(8,128)S(1)} %get-tuple-element.203, pred[]{:T(512)S(6)} %compare.4), kind=kOutput, calls=%fused_computation.4.clone.1 | convolution fusion | flops 3222011904 | bytes 5251073 | tf_op jit(solution)/shard_map/while/body/eval_jaxpr/dot_general | solution.py:88
  138.3 1.3 dynamic-slice_convert_fusion.4
  139.7 3.1 %multiply_reduce_fusion.2 = f32[8,64,2048]{2,1,0:T(8,128)} fusion(f32[3,64,2048]{2,1,0:T(8,128)S(1)} %dynamic-slice_convert_fusion.4, f32[3,8,2048]{2,1,0:T(8,128)S(1)} %dynamic-slice_convert_fusion.5), kind=kLoop, calls=%fused_computation.1.clone.1 | loop fusion | flops 5242880 | bytes 5963776 | tf_op jit(solution)/shard_map/while/body/eval_jaxpr/reduce_sum | solution.py:85
  143.4 4.7 %fusion.30 = f32[512,256]{1,0:T(8,128)S(1)} fusion(f32[512,2048]{1,0:T(8,128)} %bitcast.30, s32[2048]{0:T(1024)S(1)} %dynamic_slice.41, f32[512,256]{1,0:T(8,128)S(1)} %get-tuple-element.203, pred[]{:T(512)S(6)} %compare.4), kind=kOutput, calls=%fused_computation.4.clone.1 | convolution fusion | flops 3222011904 | bytes 5251073 | tf_op jit(solution)/shard_map/while/body/eval_jaxpr/dot_general | solution.py:88
  148.1 1.3 dynamic-slice_convert_fusion.4
  149.5 3.1 %multiply_reduce_fusion.2 = f32[8,64,2048]{2,1,0:T(8,128)} fusion(f32[3,64,2048]{2,1,0:T(8,128)S(1)} %dynamic-slice_convert_fusion.4, f32[3,8,2048]{2,1,0:T(8,128)S(1)} %dynamic-slice_convert_fusion.5), kind=kLoop, calls=%fused_computation.1.clone.1 | loop fusion | flops 5242880 | bytes 5963776 | tf_op jit(solution)/shard_map/while/body/eval_jaxpr/reduce_sum | solution.py:85
  153.3 4.7 %fusion.30 = f32[512,256]{1,0:T(8,128)S(1)} fusion(f32[512,2048]{1,0:T(8,128)} %bitcast.30, s32[2048]{0:T(1024)S(1)} %dynamic_slice.41, f32[512,256]{1,0:T(8,128)S(1)} %get-tuple-element.203, pred[]{:T(512)S(6)} %compare.4), kind=kOutput, calls=%fused_computation.4.clone.1 | convolution fusion | flops 3222011904 | bytes 5251073 | tf_op jit(solution)/shard_map/while/body/eval_jaxpr/dot_general | solution.py:88
  158.0 1.3 dynamic-slice_convert_fusion.4
  159.3 3.1 %multiply_reduce_fusion.2 = f32[8,64,2048]{2,1,0:T(8,128)} fusion(f32[3,64,2048]{2,1,0:T(8,128)S(1)} %dynamic-slice_convert_fusion.4, f32[3,8,2048]{2,1,0:T(8,128)S(1)} %dynamic-slice_convert_fusion.5), kind=kLoop, calls=%fused_computation.1.clone.1 | loop fusion | flops 5242880 | bytes 5963776 | tf_op jit(solution)/shard_map/while/body/eval_jaxpr/reduce_sum | solution.py:85
  163.1 4.7 %fusion.30 = f32[512,256]{1,0:T(8,128)S(1)} fusion(f32[512,2048]{1,0:T(8,128)} %bitcast.30, s32[2048]{0:T(1024)S(1)} %dynamic_slice.41, f32[512,256]{1,0:T(8,128)S(1)} %get-tuple-element.203, pred[]{:T(512)S(6)} %compare.4), kind=kOutput, calls=%fused_computation.4.clone.1 | convolution fusion | flops 3222011904 | bytes 5251073 | tf_op jit(solution)/shard_map/while/body/eval_jaxpr/dot_general | solution.py:88
  167.8 1.3 dynamic-slice_convert_fusion.4
  169.1 3.1 %multiply_reduce_fusion.2 = f32[8,64,2048]{2,1,0:T(8,128)} fusion(f32[3,64,2048]{2,1,0:T(8,128)S(1)} %dynamic-slice_convert_fusion.4, f32[3,8,2048]{2,1,0:T(8,128)S(1)} %dynamic-slice_convert_fusion.5), kind=kLoop, calls=%fused_computation.1.clone.1 | loop fusion | flops 5242880 | bytes 5963776 | tf_op jit(solution)/shard_map/while/body/eval_jaxpr/reduce_sum | solution.py:85
  172.9 4.7 %fusion.30 = f32[512,256]{1,0:T(8,128)S(1)} fusion(f32[512,2048]{1,0:T(8,128)} %bitcast.30, s32[2048]{0:T(1024)S(1)} %dynamic_slice.41, f32[512,256]{1,0:T(8,128)S(1)} %get-tuple-element.203, pred[]{:T(512)S(6)} %compare.4), kind=kOutput, calls=%fused_computation.4.clone.1 | convolution fusion | flops 3222011904 | bytes 5251073 | tf_op jit(solution)/shard_map/while/body/eval_jaxpr/dot_general | solution.py:88
  178.9 3.1 %multiply_reduce_fusion.2 = f32[8,64,2048]{2,1,0:T(8,128)} fusion(f32[3,64,2048]{2,1,0:T(8,128)S(1)} %dynamic-slice_convert_fusion.4, f32[3,8,2048]{2,1,0:T(8,128)S(1)} %dynamic-slice_convert_fusion.5), kind=kLoop, calls=%fused_computation.1.clone.1 | loop fusion | flops 5242880 | bytes 5963776 | tf_op jit(solution)/shard_map/while/body/eval_jaxpr/reduce_sum | solution.py:85
  182.7 4.7 %fusion.30 = f32[512,256]{1,0:T(8,128)S(1)} fusion(f32[512,2048]{1,0:T(8,128)} %bitcast.30, s32[2048]{0:T(1024)S(1)} %dynamic_slice.41, f32[512,256]{1,0:T(8,128)S(1)} %get-tuple-element.203, pred[]{:T(512)S(6)} %compare.4), kind=kOutput, calls=%fused_computation.4.clone.1 | convolution fusion | flops 3222011904 | bytes 5251073 | tf_op jit(solution)/shard_map/while/body/eval_jaxpr/dot_general | solution.py:88
  187.6 1.9 fusion.15
  190.1 74.7 %psum.7 = f32[64]{0:T(128)S(1)} all-reduce(f32[64]{0:T(128)S(1)} %dynamic_update_slice.3), channel_id=1, replica_groups=mesh['tile'=32,'mode'=8] {'tile','mode'}, use_global_device_ids=true, to_apply=%region_5.6 | all-reduce | flops 64 | bytes 512 | tf_op jit(solution)/shard_map/psum | solution.py:68
  264.9 8.6 %reduce-scatter.2.cloned.1.call-done = f32[16,512]{1,0:T(8,128)} async-done(((f32[512,512]{1,0:T(8,128)}), f32[16,512]{1,0:T(8,128)}) %reduce-scatter.2.cloned.1.call-update) | async-done | bytes 32784 | tf_op jit(solution)/shard_map/reduce_scatter | solution.py:101
  (56 shorter events, 19.1 us)
Async XLA Ops:
  6.5 14.6 %copy-start = (s32[32,32,8]{1,2,0:T(8,128)S(1)}, s32[32,32,8]{1,2,0:T(8,128)}, u32[]{:S(2)}) copy-start(s32[32,32,8]{1,2,0:T(8,128)} %param.9) | copy-start | bytes 98308
  6.5 91.9 %all-gather.2.cloned.1.call-start = ((), (), s32[]{:S(2)}) async-start(), calls=%async_computation.1 | async-start | bytes 7077888 | tf_op jit(solution)/shard_map/all_gather | solution.py:69
  7.7 7.7 %collective-permute-start = (bf16[8,1,2048]{2,1,0:T(2,128)(2,1)S(1)}, bf16[8,1,2048]{2,1,0:T(2,128)(2,1)S(1)}, u32[]{:S(2)}, u32[]{:S(2)}) collective-permute-start(bf16[8,1,2048]{2,1,0:T(2,128)(2,1)S(1)} %get-tuple-element.160), channel_id=1, source_target_pairs={{0,8},{8,16},{16,24},{24,32},{32,40},{40,48},{48,56},{56,64},{64,7... | collective-permute-start | bytes 98312 | tf_op jit(solution)/shard_map/ppermute | solution.py:20
  9.6 7.6 %collective-permute-start.1 = (bf16[8,1,2048]{2,1,0:T(2,128)(2,1)S(1)}, bf16[8,1,2048]{2,1,0:T(2,128)(2,1)S(1)}, u32[]{:S(2)}, u32[]{:S(2)}) collective-permute-start(bf16[8,1,2048]{2,1,0:T(2,128)(2,1)S(1)} %get-tuple-element.161), channel_id=1, source_target_pairs={{8,0},{16,8},{24,16},{32,24},{40,32},{48,40},{56,48},{64,56},{72,6... | collective-permute-start | bytes 98312 | tf_op jit(solution)/shard_map/ppermute | solution.py:22
  19.4 1.2 copy-start.4
  19.4 1.9 copy-start.3
  20.5 253.1 %reduce-scatter.2.cloned.1.call-start = ((), (), s32[]{:S(2)}) async-start(), calls=%async_computation.2 | async-start | bytes 1081344 | tf_op jit(solution)/shard_map/reduce_scatter | solution.py:101
  187.6 2.0 copy-start.1
  187.6 2.0 copy-start.2
Sparse Core Ops, SparseCore 0:
  20.6 77.8 all-gather.1
  189.7 83.7 reduce-scatter.1
where the time goes:
time: 283 us; the launch traced here: 282 us
  waiting for transfers between devices  82.2 us (29%)
  blocking collectives  74.7 us (26%)
  other arithmetic  42.3 us (15%)
  matrix products  39.4 us (14%)
  local copies, waits for them, and re-layouts  21.7 us (8%)
  between operations  13.5 us (5%)
  starting transfers between devices  7.72 us (3%)
    psum x1, blocking collectives, per_device(): totals = 0.5 * lax.psum(placed_sums, ('tile', 'mode'))  74.7 us
    all_gather x1, waiting for transfers between devices, per_device(): gathered_bend = lax.all_gather(own_bending, 'mode', axis=1, tiled=True)  71.7 us
    dot_general x8, matrix products, one_block(): jnp.dot(products, member_block, precision=lax.Precision.HIGHEST)  37.5 us
    reduce_sum x8, other arithmetic, one_block(): jnp.sum(left_block[:, :, None, :] * right_block[:, None, :, :], axis=0)  24.5 us
    reshape x1, local copies, waits for them, and re-layouts, per_device(): right_flat = gathered_bend.reshape(3, mode_count, node_count)  10.4 us
    convert_element_type x8, other arithmetic, one_block(): lax.dynamic_slice_in_dim(right_flat, first_node, block_nodes, 2)  10.4 us
    reduce_scatter x1, waiting for transfers between devices, per_device(): lax.psum_scatter(spread_zones, 'tile', scatter_dimension=0, tiled=True)  8.6 us
    ppermute x1, starting transfers between devices, with_halo(): lax.ppermute(head, axis, [((i + 1) % count, i) for i in range(ends)])  5.75 us
  transfers between devices with their start and end apart: 4, of which 3 were waited for; matrix products, arithmetic and copies ran while one was open for 2% of the time, Pallas kernels for 0%

commit v1 on v0

--- a/solution.py
+++ b/solution.py
@@ -66,7 +66,10 @@
         jnp.zeros((mode_count,), jnp.float32), own_sums, lax.axis_index("mode") * panel_modes, 0
     )
     totals = 0.5 * lax.psum(placed_sums, ("tile", "mode"))
-    gathered_bend = lax.all_gather(own_bending, "mode", axis=1, tiled=True)
+    size = lax.axis_size("mode")
+    blocks = jnp.stack([own_bending for _ in range(size)])
+    blocks = lax.all_to_all(blocks, "mode", split_axis=0, concat_axis=0)
+    gathered_bend = jnp.concatenate(blocks, axis=1)
     right_flat = gathered_bend.reshape(3, mode_count, node_count)
     left_flat = weighted.astype(jnp.bfloat16).reshape(3, panel_modes, node_count)
     slot_flat = node_slot.reshape(node_count)

time: 283 us -> 366 us (1.29)
  waiting for transfers between devices: 82.2 us -> 145 us
  local copies, waits for them, and re-layouts: 21.7 us -> 36 us
  starting transfers between devices: 7.72 us -> 16.5 us
    all_to_all x0 -> x1, waiting for transfers between devices: none -> 135 us  [per_device(): blocks = lax.all_to_all(blocks, 'mode', split_axis=0, concat_axis=0)]
    all_gather x1 -> x0, waiting for transfers between devices: 71.7 us -> none  [per_device(): gathered_bend = lax.all_gather(own_bending, 'mode', axis=1, tiled=True)]
    another operation x0 -> x3, local copies, waits for them, and re-layouts: none -> 14.3 us  [the longest x1 10.4 us: per_device(): right_flat = gathered_bend.reshape(3, mode_count, node_count)]
    all_to_all x0 -> x1, starting transfers between devices: none -> 8.6 us  [per_device(): blocks = lax.all_to_all(blocks, 'mode', split_axis=0, concat_axis=0)]
where the time goes in v1:
time: 366 us; the launch traced here: 364 us
  waiting for transfers between devices  145 us (40%)
  blocking collectives  72.6 us (20%)
  other arithmetic  41.5 us (11%)
  matrix products  39.4 us (11%)
  local copies, waits for them, and re-layouts  36 us (10%)
  starting transfers between devices  16.5 us (5%)
  between operations  13.5 us (4%)
    all_to_all x1, waiting for transfers between devices, per_device(): blocks = lax.all_to_all(blocks, 'mode', split_axis=0, concat_axis=0)  135 us
    psum x1, blocking collectives, per_device(): totals = 0.5 * lax.psum(placed_sums, ('tile', 'mode'))  72.6 us
    dot_general x8, matrix products, one_block(): jnp.dot(products, member_block, precision=lax.Precision.HIGHEST)  37.5 us
    reduce_sum x8, other arithmetic, one_block(): jnp.sum(left_block[:, :, None, :] * right_block[:, None, :, :], axis=0)  24.6 us
    reshape x1, local copies, waits for them, and re-layouts, per_device(): gathered_bend = jnp.concatenate(blocks, axis=1)  10.4 us
    another operation x1, local copies, waits for them, and re-layouts, per_device(): right_flat = gathered_bend.reshape(3, mode_count, node_count)  10.4 us
    convert_element_type x8, other arithmetic, one_block(): lax.dynamic_slice_in_dim(right_flat, first_node, block_nodes, 2)  10.4 us
    all_to_all x1, starting transfers between devices, per_device(): blocks = lax.all_to_all(blocks, 'mode', split_axis=0, concat_axis=0)  8.6 us
  transfers between devices with their start and end apart: 4, of which 3 were waited for; matrix products, arithmetic and copies ran while one was open for 2% of the time, Pallas kernels for 0%

profile of v1, /device:TPU:4, one launch (start us, length us, event | category | flops | bytes accessed | tf_op | source)
XLA Modules:
  0.0 364.4 jit_solution(7498594519757578848)
XLA Ops:
  7.7 1.9 collective-permute-start
  9.6 5.8 %collective-permute-start.1 = (bf16[8,1,2048]{2,1,0:T(2,128)(2,1)S(1)}, bf16[8,1,2048]{2,1,0:T(2,128)(2,1)S(1)}, u32[]{:S(2)}, u32[]{:S(2)}) collective-permute-start(bf16[8,1,2048]{2,1,0:T(2,128)(2,1)S(1)} %get-tuple-element.161), channel_id=1, source_target_pairs={{8,0},{16,8},{24,16},{32,24},{40,32},{48,40},{56,48},{64,56},{72,6... | collective-permute-start | bytes 98312 | tf_op jit(solution)/shard_map/ppermute | solution.py:22
  15.4 1.9 collective-permute-done.1
  20.0 3.5 stack.49
  23.4 8.6 %all-to-all-start = ((bf16[8,3,8,8,2048]{4,2,3,1,0:T(8,128)(2,1)}), bf16[8,3,8,8,2048]{4,2,3,1,0:T(8,128)(2,1)}, u32[]{:S(2)}, u32[]{:S(2)}) async-start(bf16[8,3,8,8,2048]{4,2,3,1,0:T(8,128)(2,1)} %stack.49), calls=%async_computation | async-start | bytes 12582912 | tf_op jit(solution)/shard_map/all_to_all | solution.py:71
  33.0 2.2 fusion.22
  38.6 134.8 %all-to-all-done = bf16[8,3,8,8,2048]{4,2,3,1,0:T(8,128)(2,1)} async-done(((bf16[8,3,8,8,2048]{4,2,3,1,0:T(8,128)(2,1)}), bf16[8,3,8,8,2048]{4,2,3,1,0:T(8,128)(2,1)}, u32[]{:S(2)}, u32[]{:S(2)}) %all-to-all-start) | async-done | bytes 6291488 | tf_op jit(solution)/shard_map/all_to_all | solution.py:71
  173.4 10.4 %copy.19 = bf16[3,8,8,8,2048]{4,3,2,1,0:T(8,128)(2,1)} copy(bf16[3,8,8,8,2048]{4,2,3,0,1:T(8,128)(2,1)} %bitcast.4) | data formatting | bytes 12582912 | tf_op jit(solution)/shard_map/reshape | solution.py:72
  183.8 10.4 %reshape_reshape.3 = bf16[3,64,16384]{2,1,0:T(8,128)(2,1)} reshape(bf16[3,8,8,8,2048]{4,3,2,1,0:T(8,128)(2,1)} %copy.19) | data formatting | bytes 12582912 | tf_op jit(solution)/shard_map/reshape;reshape | solution.py:73
  194.2 78.5 %while.14 = (s32[]{:T(128)}, f32[512,256]{1,0:T(8,128)S(1)}, bf16[3,8,16384]{2,1,0:T(8,128)(2,1)S(1)}, bf16[3,64,16384]{2,1,0:T(8,128)(2,1)}, s32[16384]{0:T(102...) while((s32[]{:T(128)}, f32[512,256]{1,0:T(8,128)S(1)}, bf16[3,8,16384]{2,1,0:T(8,128)(2,1)S(1)}, ...), condition=%wide.region_2.3_spmd.clone, body=%wide.region_0.0_spmd.clone.sunk | while | flops 3227697152 | bytes 13885601 | solution.py:93
  195.5 3.1 multiply_reduce_fusion.2
  199.3 4.7 %fusion.30 = f32[512,256]{1,0:T(8,128)S(1)} fusion(f32[512,2048]{1,0:T(8,128)} %bitcast.31, s32[2048]{0:T(1024)S(1)} %dynamic_slice.41, f32[512,256]{1,0:T(8,128)S(1)} %get-tuple-element.203, pred[]{:T(512)S(6)} %compare.4), kind=kOutput, calls=%fused_computation.4.clone.1 | convolution fusion | flops 3222011904 | bytes 5251073 | tf_op jit(solution)/shard_map/while/body/eval_jaxpr/dot_general | solution.py:91
  204.0 1.3 dynamic-slice_convert_fusion.4
  205.3 3.1 multiply_reduce_fusion.2
  209.1 4.7 %fusion.30 = f32[512,256]{1,0:T(8,128)S(1)} fusion(f32[512,2048]{1,0:T(8,128)} %bitcast.31, s32[2048]{0:T(1024)S(1)} %dynamic_slice.41, f32[512,256]{1,0:T(8,128)S(1)} %get-tuple-element.203, pred[]{:T(512)S(6)} %compare.4), kind=kOutput, calls=%fused_computation.4.clone.1 | convolution fusion | flops 3222011904 | bytes 5251073 | tf_op jit(solution)/shard_map/while/body/eval_jaxpr/dot_general | solution.py:91
  213.8 1.3 dynamic-slice_convert_fusion.4
  215.2 3.1 multiply_reduce_fusion.2
  218.9 4.7 %fusion.30 = f32[512,256]{1,0:T(8,128)S(1)} fusion(f32[512,2048]{1,0:T(8,128)} %bitcast.31, s32[2048]{0:T(1024)S(1)} %dynamic_slice.41, f32[512,256]{1,0:T(8,128)S(1)} %get-tuple-element.203, pred[]{:T(512)S(6)} %compare.4), kind=kOutput, calls=%fused_computation.4.clone.1 | convolution fusion | flops 3222011904 | bytes 5251073 | tf_op jit(solution)/shard_map/while/body/eval_jaxpr/dot_general | solution.py:91
  223.6 1.3 dynamic-slice_convert_fusion.4
  225.0 3.1 multiply_reduce_fusion.2
  228.8 4.7 %fusion.30 = f32[512,256]{1,0:T(8,128)S(1)} fusion(f32[512,2048]{1,0:T(8,128)} %bitcast.31, s32[2048]{0:T(1024)S(1)} %dynamic_slice.41, f32[512,256]{1,0:T(8,128)S(1)} %get-tuple-element.203, pred[]{:T(512)S(6)} %compare.4), kind=kOutput, calls=%fused_computation.4.clone.1 | convolution fusion | flops 3222011904 | bytes 5251073 | tf_op jit(solution)/shard_map/while/body/eval_jaxpr/dot_general | solution.py:91
  234.8 3.1 multiply_reduce_fusion.2
  238.6 4.7 %fusion.30 = f32[512,256]{1,0:T(8,128)S(1)} fusion(f32[512,2048]{1,0:T(8,128)} %bitcast.31, s32[2048]{0:T(1024)S(1)} %dynamic_slice.41, f32[512,256]{1,0:T(8,128)S(1)} %get-tuple-element.203, pred[]{:T(512)S(6)} %compare.4), kind=kOutput, calls=%fused_computation.4.clone.1 | convolution fusion | flops 3222011904 | bytes 5251073 | tf_op jit(solution)/shard_map/while/body/eval_jaxpr/dot_general | solution.py:91
  244.6 3.1 multiply_reduce_fusion.2
  248.4 4.7 %fusion.30 = f32[512,256]{1,0:T(8,128)S(1)} fusion(f32[512,2048]{1,0:T(8,128)} %bitcast.31, s32[2048]{0:T(1024)S(1)} %dynamic_slice.41, f32[512,256]{1,0:T(8,128)S(1)} %get-tuple-element.203, pred[]{:T(512)S(6)} %compare.4), kind=kOutput, calls=%fused_computation.4.clone.1 | convolution fusion | flops 3222011904 | bytes 5251073 | tf_op jit(solution)/shard_map/while/body/eval_jaxpr/dot_general | solution.py:91
  254.4 3.1 multiply_reduce_fusion.2
  258.2 4.7 %fusion.30 = f32[512,256]{1,0:T(8,128)S(1)} fusion(f32[512,2048]{1,0:T(8,128)} %bitcast.31, s32[2048]{0:T(1024)S(1)} %dynamic_slice.41, f32[512,256]{1,0:T(8,128)S(1)} %get-tuple-element.203, pred[]{:T(512)S(6)} %compare.4), kind=kOutput, calls=%fused_computation.4.clone.1 | convolution fusion | flops 3222011904 | bytes 5251073 | tf_op jit(solution)/shard_map/while/body/eval_jaxpr/dot_general | solution.py:91
  264.3 3.1 multiply_reduce_fusion.2
  268.0 4.7 %fusion.30 = f32[512,256]{1,0:T(8,128)S(1)} fusion(f32[512,2048]{1,0:T(8,128)} %bitcast.31, s32[2048]{0:T(1024)S(1)} %dynamic_slice.41, f32[512,256]{1,0:T(8,128)S(1)} %get-tuple-element.203, pred[]{:T(512)S(6)} %compare.4), kind=kOutput, calls=%fused_computation.4.clone.1 | convolution fusion | flops 3222011904 | bytes 5251073 | tf_op jit(solution)/shard_map/while/body/eval_jaxpr/dot_general | solution.py:91
  273.0 1.9 fusion.15
  275.4 72.6 %psum.7 = f32[64]{0:T(128)S(1)} all-reduce(f32[64]{0:T(128)S(1)} %dynamic_update_slice.3), channel_id=1, replica_groups=mesh['tile'=32,'mode'=8] {'tile','mode'}, use_global_device_ids=true, to_apply=%region_5.6 | all-reduce | flops 64 | bytes 512 | tf_op jit(solution)/shard_map/psum | solution.py:68
  348.2 7.9 %reduce-scatter.2.cloned.1.call-done = f32[16,512]{1,0:T(8,128)} async-done(((f32[512,512]{1,0:T(8,128)}), f32[16,512]{1,0:T(8,128)}) %reduce-scatter.2.cloned.1.call-update) | async-done | bytes 32784 | tf_op jit(solution)/shard_map/reduce_scatter | solution.py:104
  (58 shorter events, 22.7 us)
Async XLA Ops:
  6.5 26.4 %copy-start = (s32[32,32,8]{1,2,0:T(8,128)S(1)}, s32[32,32,8]{1,2,0:T(8,128)}, u32[]{:S(2)}) copy-start(s32[32,32,8]{1,2,0:T(8,128)} %param.9) | copy-start | bytes 98308
  7.7 7.7 %collective-permute-start = (bf16[8,1,2048]{2,1,0:T(2,128)(2,1)S(1)}, bf16[8,1,2048]{2,1,0:T(2,128)(2,1)S(1)}, u32[]{:S(2)}, u32[]{:S(2)}) collective-permute-start(bf16[8,1,2048]{2,1,0:T(2,128)(2,1)S(1)} %get-tuple-element.160), channel_id=1, source_target_pairs={{0,8},{8,16},{16,24},{24,32},{32,40},{40,48},{48,56},{56,64},{64,7... | collective-permute-start | bytes 98312 | tf_op jit(solution)/shard_map/ppermute | solution.py:20
  9.6 7.6 %collective-permute-start.1 = (bf16[8,1,2048]{2,1,0:T(2,128)(2,1)S(1)}, bf16[8,1,2048]{2,1,0:T(2,128)(2,1)S(1)}, u32[]{:S(2)}, u32[]{:S(2)}) collective-permute-start(bf16[8,1,2048]{2,1,0:T(2,128)(2,1)S(1)} %get-tuple-element.161), channel_id=1, source_target_pairs={{8,0},{16,8},{24,16},{32,24},{40,32},{48,40},{56,48},{64,56},{72,6... | collective-permute-start | bytes 98312 | tf_op jit(solution)/shard_map/ppermute | solution.py:22
  23.4 8.8 %copy-start.4 = (s32[8,2048]{1,0:T(8,128)S(1)}, s32[8,2048]{1,0:T(8,128)}, u32[]{:S(2)}) copy-start(s32[8,2048]{1,0:T(8,128)} %param.8) | copy-start | bytes 196612
  23.4 9.6 %copy-start.3 = (f32[8,2048]{1,0:T(8,128)S(1)}, f32[8,2048]{1,0:T(8,128)}, u32[]{:S(2)}) copy-start(f32[8,2048]{1,0:T(8,128)} %param.7) | copy-start | bytes 196612
  23.4 149.9 %all-to-all-start = ((bf16[8,3,8,8,2048]{4,2,3,1,0:T(8,128)(2,1)}), bf16[8,3,8,8,2048]{4,2,3,1,0:T(8,128)(2,1)}, u32[]{:S(2)}, u32[]{:S(2)}) async-start(bf16[8,3,8,8,2048]{4,2,3,1,0:T(8,128)(2,1)} %stack.49), calls=%async_computation | async-start | bytes 12582912 | tf_op jit(solution)/shard_map/all_to_all | solution.py:71
  32.0 324.1 %reduce-scatter.2.cloned.1.call-start = ((), (), s32[]{:S(2)}) async-start(), calls=%async_computation.2 | async-start | bytes 1081344 | tf_op jit(solution)/shard_map/reduce_scatter | solution.py:104
  272.7 2.2 copy-start.1
  272.7 2.2 copy-start.2
Sparse Core Ops, SparseCore 0:
  275.0 81.0 reduce-scatter.1
